TPU v7x, 32 devices: a whole 2x2x4 slice. The times are simulated.
32 devices in a mesh: head: 4 (over x, core), ctx: 8 (over z, y).
Axes of the slice: x: 2, y: 2, z: 4, core: 2. Of those that a mesh axis runs over, the one named last changes fastest.
Arguments:
- q_in: bfloat16 [2048, 2048], P('ctx', 'head'), may hold values from -6 to 6
- k_in: bfloat16 [2048, 2048], P('ctx', 'head'), may hold values from -6 to 6
- v_in: bfloat16 [2048, 4096], P('ctx', 'head'), may hold values from -6 to 6
- gate_in: bfloat16 [2048, 4096], P('ctx', 'head'), may hold values from -6 to 6
- conv_q: float32 [4, 2048], P(None, 'head'), may hold values from -3 to 3
- conv_k: float32 [4, 2048], P(None, 'head'), may hold values from -3 to 3
- value_conv_taps: float32 [4, 4096], P(None, 'head'), may hold values from -3 to 3
- a_in: float32 [32, 2048], P('head', 'ctx'), may hold values from -4 to 12.1
- b_in: float32 [32, 2048], P('head', 'ctx'), may hold values from -5.3 to 1
- a_log: float32 [32], P('head'), may hold values from -0.92 to 0
- dt_bias: float32 [32], P('head'), may hold values from -12.5 to -3.4
- norm_gain: float32 [128], replicated, may hold values from 0.5 to 1.5
- out_weight: bfloat16 [4096, 2048], P('head'), may hold values from -0.125 to 0.125
Outputs:
- layer_out: bfloat16 [2048, 2048], P('ctx', 'head')
All inputs are finite; a program needn't handle non-finite values.
Results may differ from a plain program's by a relative error of at most 0.0049.
Values may be sent and summed in bfloat16 or wider, within the bound.
A program may use at most 128 MiB of HBM per device.

v0:
```python
import functools

import jax
import jax.numpy as jnp
from jax import lax
from jax.experimental import pallas as pl
from jax.experimental.pallas import tpu as pltpu
from jax.sharding import PartitionSpec as P

KH = 16
VH = 32
DK = 128
DV = 128
RATIO = VH // KH
F32 = jnp.float32
BF16 = jnp.bfloat16
NN = (((1,), (0,)), ((), ()))
NT = (((1,), (1,)), ((), ()))
TN = (((0,), (0,)), ((), ()))


def shifted(block, axis, distance):
    devices = range(lax.axis_size(axis))
    route = [(i - distance, i) for i in devices if i - distance in devices]
    return lax.ppermute(block, axis, route)


def mm1(left, right, dims=NN):
    return lax.dot_general(left.astype(BF16), right.astype(BF16), dims, preferred_element_type=F32)


def split(x):
    high = x.astype(BF16)
    return high, (x - high.astype(F32)).astype(BF16)


def mm3(left, right, dims=NN):
    lh, ll = split(left)
    rh, rl = split(right)
    return mm1(lh, rh, dims) + (mm1(lh, rl, dims) + mm1(ll, rh, dims))


def exact_left(mask, right, dims):
    high, low = split(right)
    rest = (right - high.astype(F32) - low.astype(F32)).astype(BF16)
    return mm1(mask, high, dims) + (mm1(mask, low, dims) + mm1(mask, rest, dims))


def silu(x):
    return x / (1.0 + jnp.exp(-x))


def conv(x, halo, taps, ext):
    length, width = x.shape
    ext[0:8, :width] = jnp.zeros((8, width), F32)
    ext[5:8, :width] = halo.astype(F32)
    ext[8 : 8 + length, :width] = x.astype(F32)
    total = taps[0:1] * ext[5 : 5 + length, :width]
    for j in range(1, 4):
        total = total + taps[j : j + 1] * ext[5 + j : 5 + j + length, :width]
    return silu(total)


def unit(x):
    return x * lax.rsqrt(jnp.sum(x * x, axis=-1, keepdims=True) + 1e-06)


def local_terms(q, k, v, a2, b2, alog2, dt2):
    n = q.shape[0]
    row = lax.broadcasted_iota(jnp.int32, (n, n), 0)
    col = lax.broadcasted_iota(jnp.int32, (n, n), 1)
    lower = row >= col
    strict = row > col
    xor = row ^ col
    tri = jnp.where(lower, 1.0, 0.0)
    eye = jnp.where(row == col, 1.0, 0.0)
    x = a2 + dt2
    ld = -jnp.exp(alog2) * (jnp.maximum(x, 0.0) + jnp.log1p(jnp.exp(-jnp.abs(x))))
    strength = 1.0 / (1.0 + jnp.exp(-b2))
    ldh, ldl = split(ld)
    c_row = (
        mm1(ldh, tri, NT)
        + mm1(ldl, tri, NT)
        + mm1(ld - ldh.astype(F32) - ldl.astype(F32), tri, NT)
    )
    c_col = exact_left(tri, ld, NT)
    b_col = exact_left(eye, strength, NT)
    kk = mm3(k, k, NT)
    qk = mm3(q, k, NT)
    results = []
    for r in range(RATIO):
        cc = c_col[:, r : r + 1]
        bc = b_col[:, r : r + 1]
        gap = cc - c_row[r : r + 1, :]
        damp = jnp.where(lower, jnp.exp(jnp.minimum(gap, 0.0)), 0.0)
        low = jnp.where(strict, bc * kk * damp, 0.0)
        inv = eye - jnp.where(xor == 1, low, 0.0)
        span = 2
        while span < n:
            off = jnp.where((xor >= span) & (xor < 2 * span), low, 0.0).astype(BF16)
            inv_b = inv.astype(BF16)
            inv = inv - mm1(mm1(inv_b, off), inv_b)
            span *= 2
        inv_b = inv.astype(BF16)
        gate = jnp.exp(cc)
        rhs = jnp.concatenate([bc * gate * k, bc * v[:, r * DV : (r + 1) * DV]], axis=1)
        y = mm1(inv_b, rhs)
        y = y + mm1(inv_b, rhs - y - mm3(low, y))
        sy = mm3(qk * damp, y)
        last = cc[n - 1 : n]
        ky = mm3(jnp.exp(last - cc) * k, y, TN)
        results.append((gate * q - sy[:, :DK], sy[:, DK:], ky[:, :DK], ky[:, DK:], jnp.exp(last)))
    return results


def pick_rows(x, g):
    index = lax.broadcasted_iota(jnp.int32, x.shape, 0)
    rows = [jnp.sum(jnp.where(index == g * RATIO + r, x, 0.0), axis=0, keepdims=True) for r in range(RATIO)]
    return jnp.concatenate(rows, axis=0)


def k1_body(q_ref, k_ref, v_ref, hq_ref, hk_ref, hv_ref, cq_ref, ck_ref, cv_ref, a_ref, b_ref,
            alog_ref, dt_ref, qe_ref, o_ref, m_ref, bb_ref, ext):
    g = pl.program_id(0)
    n = q_ref.shape[0]
    q = unit(conv(q_ref[...], hq_ref[...], cq_ref[...], ext)) * DK ** (-0.5)
    k = unit(conv(k_ref[...], hk_ref[...], ck_ref[...], ext))
    v = conv(v_ref[...], hv_ref[...], cv_ref[...], ext)
    a2 = pick_rows(a_ref[...], g)
    b2 = pick_rows(b_ref[...], g)
    alog2 = jnp.concatenate([jnp.full((1, n), alog_ref[g * RATIO + r], F32) for r in range(RATIO)], axis=0)
    dt2 = jnp.concatenate([jnp.full((1, n), dt_ref[g * RATIO + r], F32) for r in range(RATIO)], axis=0)
    terms = local_terms(q, k, v, a2, b2, alog2, dt2)
    eye = jnp.where(
        lax.broadcasted_iota(jnp.int32, (DK, DK), 0) == lax.broadcasted_iota(jnp.int32, (DK, DK), 1), 1.0, 0.0
    )
    for r, (qe, o, d, bb, gl) in enumerate(terms):
        qe_ref[:, r * DV : (r + 1) * DV] = qe
        o_ref[:, r * DV : (r + 1) * DV] = o
        m_ref[r] = gl * eye - d
        bb_ref[r] = bb


def matmul_hi(left, right):
    return jnp.einsum("...ij,...jk->...ik", left, right, precision=lax.Precision.HIGHEST)


def gated_norm(core, gate_in, norm_gain):
    scale_rows = lax.rsqrt(jnp.mean(core * core, axis=-1, keepdims=True) + 1e-06)
    gate_vals = gate_in.astype(F32).reshape(core.shape)
    normalized_rows = core * scale_rows * norm_gain * jax.nn.silu(gate_vals)
    return normalized_rows.astype(BF16).reshape(core.shape[0], -1)


def local(q_in, k_in, v_in, gate_in, conv_q, conv_k, value_conv_taps, a_in, b_in, a_log, dt_bias,
          norm_gain, out_weight):
    n = q_in.shape[0]
    khl = q_in.shape[1] // DK
    vhl = v_in.shape[1] // DV
    tails = jnp.concatenate([q_in[n - 3 :], k_in[n - 3 :], v_in[n - 3 :]], axis=1)
    before = shifted(tails, "ctx", 1)
    vw = RATIO * DV
    smem = pl.BlockSpec(memory_space=pltpu.SMEM)
    qe, o, m, bb = pl.pallas_call(
        k1_body,
        grid=(khl,),
        in_specs=[
            pl.BlockSpec((n, DK), lambda g: (0, g)),
            pl.BlockSpec((n, DK), lambda g: (0, g)),
            pl.BlockSpec((n, vw), lambda g: (0, g)),
            pl.BlockSpec((3, DK), lambda g: (0, g)),
            pl.BlockSpec((3, DK), lambda g: (0, khl + g)),
            pl.BlockSpec((3, vw), lambda g: (0, khl + g)),
            pl.BlockSpec((4, DK), lambda g: (0, g)),
            pl.BlockSpec((4, DK), lambda g: (0, g)),
            pl.BlockSpec((4, vw), lambda g: (0, g)),
            pl.BlockSpec((vhl, n), lambda g: (0, 0)),
            pl.BlockSpec((vhl, n), lambda g: (0, 0)),
            smem,
            smem,
        ],
        out_specs=[
            pl.BlockSpec((n, vw), lambda g: (0, g)),
            pl.BlockSpec((n, vw), lambda g: (0, g)),
            pl.BlockSpec((RATIO, DK, DK), lambda g: (g, 0, 0)),
            pl.BlockSpec((RATIO, DK, DV), lambda g: (g, 0, 0)),
        ],
        out_shape=[
            jax.ShapeDtypeStruct((n, vhl * DV), F32),
            jax.ShapeDtypeStruct((n, vhl * DV), F32),
            jax.ShapeDtypeStruct((vhl, DK, DK), F32),
            jax.ShapeDtypeStruct((vhl, DK, DV), F32),
        ],
        scratch_shapes=[pltpu.VMEM((n + 8, vw), F32)],
        compiler_params=pltpu.CompilerParams(vmem_limit_bytes=40 << 20),
    )(q_in, k_in, v_in, before, before, before, conv_q, conv_k, value_conv_taps, a_in, b_in, a_log, dt_bias)

    def relay(index_now, incoming):
        return shifted(matmul_hi(m, incoming) + bb, "ctx", 1)

    start = lax.fori_loop(0, lax.axis_size("ctx") - 1, relay, jnp.zeros((vhl, DK, DV), F32))
    core = jnp.einsum("thd,hde->the", qe.reshape(n, vhl, DK), start, precision=lax.Precision.HIGHEST)
    core = core + o.reshape(n, vhl, DV)
    gated = gated_norm(core, gate_in, norm_gain)
    partial_sum = jnp.dot(gated, out_weight, preferred_element_type=F32)
    return lax.psum_scatter(partial_sum, "head", scatter_dimension=1, tiled=True).astype(BF16)


def solution(mesh):
    return jax.shard_map(
        local,
        mesh=mesh,
        in_specs=(
            P("ctx", "head"),
            P("ctx", "head"),
            P("ctx", "head"),
            P("ctx", "head"),
            P(None, "head"),
            P(None, "head"),
            P(None, "head"),
            P("head", "ctx"),
            P("head", "ctx"),
            P("head"),
            P("head"),
            P(),
            P("head", None),
        ),
        out_specs=P("ctx", "head"),
        check_vma=False,
    )
```

profile of v0, /device:TPU:29, one launch (start us, length us, event | category | flops | bytes accessed | tf_op | source)
XLA Modules:
  0.0 192.9 jit_solution(10946271411113127434)
XLA Ops:
  6.5 0.7 slice.11
  7.3 0.7 slice.10
  8.0 0.7 slice.9
  8.7 1.3 collective-permute-start.1
  10.0 2.2 %copy.17 = f32[256,1024]{0,1:T(8,128)} copy(bf16[256,1024]{1,0:T(8,128)(2,1)} %param.18) | data formatting | bytes 1572864 | tf_op jit(solution)/shard_map/reshape | solution.py:150
  12.2 1.0 collective-permute-done.1.hq_ref.hk_ref.hv_ref
  13.2 1.0 copy-done
  14.2 0.9 copy-done.1
  15.2 0.9 copy-done.2
  16.1 0.7 copy-done.3
  16.8 0.7 copy-done.4
  20.9 25.3 %shard_map.127 = (f32[256,1024]{1,0:T(8,128)S(1)}, f32[256,1024]{1,0:T(8,128)S(1)}, f32[8,128,128]{2,1,0:T(8,128)S(1)}, f32[8,128,128]{2,1,0:T(8,128)S(1)}) custom-call(bf16[256,512]{1,0:T(8,128)(2,1)S(1)} %copy-done.1, bf16[256,512]{1,0:T(8,128)(2,1)S(1)} %copy-done.2, bf16[256,1024]{1,0:T(8,128)(2,1)S(1)} %copy-done, ...), custom_call_target="tpu_custom_call" | custom-call | tf_op jit(solution)/shard_map/pallas_call | solution.py:164
  46.3 1.3 copy.19
  47.7 88.9 %while.10 = (s32[]{:T(128)}, f32[8,128,128]{2,1,0:T(8,128)S(1)}, f32[8,128,128]{2,1,0:T(8,128)S(1)}, f32[8,128,128]{2,1,0:T(8,128)S(1)}, s32[]{:T(128)}) while((s32[]{:T(128)}, f32[8,128,128]{2,1,0:T(8,128)S(1)}, f32[8,128,128]{2,1,0:T(8,128)S(1)}, f32[8,128,128]{2,1,0:T(8,128)S(1)}, s32[]{:T(128)}) %tuple.19), condition=%wide.region_1.0_spmd, body=%wide.region_0.0_spmd.sunk | while | flops 201457664 | bytes 4194405 | solution.py:201
  48.3 1.3 collective-permute-start
  49.6 12.2 %collective-permute-done = f32[8,128,128]{2,1,0:T(8,128)S(1)} collective-permute-done((f32[8,128,128]{2,1,0:T(8,128)S(1)}, f32[8,128,128]{2,1,0:T(8,128)S(1)}, u32[]{:S(2)}, u32[]{:S(2)}) %collective-permute-start) | collective-permute-done | bytes 524320 | tf_op jit(solution)/shard_map/while/body/eval_jaxpr/ppermute | solution.py:25
  62.5 1.3 collective-permute-start
  63.8 12.1 %collective-permute-done = f32[8,128,128]{2,1,0:T(8,128)S(1)} collective-permute-done((f32[8,128,128]{2,1,0:T(8,128)S(1)}, f32[8,128,128]{2,1,0:T(8,128)S(1)}, u32[]{:S(2)}, u32[]{:S(2)}) %collective-permute-start) | collective-permute-done | bytes 524320 | tf_op jit(solution)/shard_map/while/body/eval_jaxpr/ppermute | solution.py:25
  76.6 1.3 collective-permute-start
  77.9 11.2 %collective-permute-done = f32[8,128,128]{2,1,0:T(8,128)S(1)} collective-permute-done((f32[8,128,128]{2,1,0:T(8,128)S(1)}, f32[8,128,128]{2,1,0:T(8,128)S(1)}, u32[]{:S(2)}, u32[]{:S(2)}) %collective-permute-start) | collective-permute-done | bytes 524320 | tf_op jit(solution)/shard_map/while/body/eval_jaxpr/ppermute | solution.py:25
  89.8 1.3 collective-permute-start
  91.1 10.3 %collective-permute-done = f32[8,128,128]{2,1,0:T(8,128)S(1)} collective-permute-done((f32[8,128,128]{2,1,0:T(8,128)S(1)}, f32[8,128,128]{2,1,0:T(8,128)S(1)}, u32[]{:S(2)}, u32[]{:S(2)}) %collective-permute-start) | collective-permute-done | bytes 524320 | tf_op jit(solution)/shard_map/while/body/eval_jaxpr/ppermute | solution.py:25
  102.0 1.3 collective-permute-start
  103.3 9.2 %collective-permute-done = f32[8,128,128]{2,1,0:T(8,128)S(1)} collective-permute-done((f32[8,128,128]{2,1,0:T(8,128)S(1)}, f32[8,128,128]{2,1,0:T(8,128)S(1)}, u32[]{:S(2)}, u32[]{:S(2)}) %collective-permute-start) | collective-permute-done | bytes 524320 | tf_op jit(solution)/shard_map/while/body/eval_jaxpr/ppermute | solution.py:25
  113.2 1.3 collective-permute-start
  114.5 9.5 %collective-permute-done = f32[8,128,128]{2,1,0:T(8,128)S(1)} collective-permute-done((f32[8,128,128]{2,1,0:T(8,128)S(1)}, f32[8,128,128]{2,1,0:T(8,128)S(1)}, u32[]{:S(2)}, u32[]{:S(2)}) %collective-permute-start) | collective-permute-done | bytes 524320 | tf_op jit(solution)/shard_map/while/body/eval_jaxpr/ppermute | solution.py:25
  124.7 1.3 collective-permute-start
  126.0 10.5 %collective-permute-done = f32[8,128,128]{2,1,0:T(8,128)S(1)} collective-permute-done((f32[8,128,128]{2,1,0:T(8,128)S(1)}, f32[8,128,128]{2,1,0:T(8,128)S(1)}, u32[]{:S(2)}, u32[]{:S(2)}) %collective-permute-start) | collective-permute-done | bytes 524320 | tf_op jit(solution)/shard_map/while/body/eval_jaxpr/ppermute | solution.py:25
  136.6 2.5 %multiply_reduce_fusion = (f32[256,8]{0,1:T(8,128)S(1)}, f32[256,8,128]{0,2,1:T(8,128)S(1)}) fusion(f32[256,8,128]{0,2,1:T(8,128)} %bitcast.27, f32[8,128,128]{2,1,0:T(8,128)S(1)} %get-tuple-element.33, f32[256,1024]{1,0:T(8,128)S(1)} %get-tuple-element.34), kind=kOutput, calls=%fused_computation.6 | convolution fusion | flops 403437568 | bytes 3678208 | tf_op jit(solution)/shard_map/thd,hde->the/dot_general | solution.py:202
  139.6 2.6 %fusion.5 = f32[256,2048]{1,0:T(8,128)} fusion(bf16[256,1024]{0,1:T(8,128)(2,1)S(1)} %bitcast.29, bf16[1024,2048]{1,0:T(8,128)(2,1)S(1)} %copy-done.12), kind=kOutput, calls=%fused_computation.9 | convolution fusion | flops 1073741824 | bytes 6815744 | tf_op jit(solution)/shard_map/dot_general | solution.py:205
  142.2 42.1 %reduce-scatter.2.cloned.1.call-done = f32[256,512]{1,0:T(8,128)} async-done(((f32[256,2048]{1,0:T(8,128)}), f32[256,512]{1,0:T(8,128)}) %reduce-scatter.2.cloned.1.call-update) | async-done | bytes 524304 | tf_op jit(solution)/shard_map/reduce_scatter | solution.py:206
  184.3 1.8 convert_element_type.8
  (34 shorter events, 8.5 us)
Async XLA Ops:
  6.5 177.8 %reduce-scatter.2.cloned.1.call-start = ((), (), s32[]{:S(2)}) async-start(), calls=%async_computation.1 | async-start | bytes 2621440 | tf_op jit(solution)/shard_map/reduce_scatter | solution.py:206
  8.7 4.5 %collective-permute-start.1 = (bf16[3,2048]{1,0:T(4,128)(2,1)S(1)}, bf16[3,2048]{1,0:T(4,128)(2,1)S(1)}, u32[]{:S(2)}, u32[]{:S(2)}) collective-permute-start(bf16[3,2048]{1,0:T(4,128)(2,1)S(1)} %pad_maximum_fusion), channel_id=1, source_target_pairs={{0,1},{1,2},{2,3},{3,4},{4,5},{5,6},{6,7},{8,9},{9,10},{10,11},{11... | collective-permute-start | bytes 36872 | tf_op jit(solution)/shard_map/ppermute | solution.py:25
  13.2 1.0 copy-start
  14.2 0.9 copy-start.1
  15.2 0.9 copy-start.2
  16.1 0.7 copy-start.3
  16.8 0.7 copy-start.4
  17.5 0.7 copy-start.5
  18.2 0.7 copy-start.6
  18.9 0.7 copy-start.7
  19.6 0.7 copy-start.8
  20.3 0.7 copy-start.9
  47.6 91.4 %copy-start.11 = (f32[128]{0:T(128)S(1)}, f32[128]{0:T(128)}, u32[]{:S(2)}) copy-start(f32[128]{0:T(128)} %param.26) | copy-start | bytes 1540
  48.3 13.5 %collective-permute-start = (f32[8,128,128]{2,1,0:T(8,128)S(1)}, f32[8,128,128]{2,1,0:T(8,128)S(1)}, u32[]{:S(2)}, u32[]{:S(2)}) collective-permute-start(f32[8,128,128]{2,1,0:T(8,128)S(1)} %convolution_add_fusion.2), channel_id=1, source_target_pairs={{0,1},{1,2},{2,3},{3,4},{4,5},{5,6},{6,7},{8,9},{9,10},{10,11},{11... | collective-permute-start | bytes 1572872 | tf_op jit(solution)/shard_map/while/body/eval_jaxpr/ppermute | solution.py:25
  62.5 13.4 %collective-permute-start = (f32[8,128,128]{2,1,0:T(8,128)S(1)}, f32[8,128,128]{2,1,0:T(8,128)S(1)}, u32[]{:S(2)}, u32[]{:S(2)}) collective-permute-start(f32[8,128,128]{2,1,0:T(8,128)S(1)} %convolution_add_fusion.2), channel_id=1, source_target_pairs={{0,1},{1,2},{2,3},{3,4},{4,5},{5,6},{6,7},{8,9},{9,10},{10,11},{11... | collective-permute-start | bytes 1572872 | tf_op jit(solution)/shard_map/while/body/eval_jaxpr/ppermute | solution.py:25
  76.6 12.5 %collective-permute-start = (f32[8,128,128]{2,1,0:T(8,128)S(1)}, f32[8,128,128]{2,1,0:T(8,128)S(1)}, u32[]{:S(2)}, u32[]{:S(2)}) collective-permute-start(f32[8,128,128]{2,1,0:T(8,128)S(1)} %convolution_add_fusion.2), channel_id=1, source_target_pairs={{0,1},{1,2},{2,3},{3,4},{4,5},{5,6},{6,7},{8,9},{9,10},{10,11},{11... | collective-permute-start | bytes 1572872 | tf_op jit(solution)/shard_map/while/body/eval_jaxpr/ppermute | solution.py:25
  89.8 11.6 %collective-permute-start = (f32[8,128,128]{2,1,0:T(8,128)S(1)}, f32[8,128,128]{2,1,0:T(8,128)S(1)}, u32[]{:S(2)}, u32[]{:S(2)}) collective-permute-start(f32[8,128,128]{2,1,0:T(8,128)S(1)} %convolution_add_fusion.2), channel_id=1, source_target_pairs={{0,1},{1,2},{2,3},{3,4},{4,5},{5,6},{6,7},{8,9},{9,10},{10,11},{11... | collective-permute-start | bytes 1572872 | tf_op jit(solution)/shard_map/while/body/eval_jaxpr/ppermute | solution.py:25
  102.0 10.5 %collective-permute-start = (f32[8,128,128]{2,1,0:T(8,128)S(1)}, f32[8,128,128]{2,1,0:T(8,128)S(1)}, u32[]{:S(2)}, u32[]{:S(2)}) collective-permute-start(f32[8,128,128]{2,1,0:T(8,128)S(1)} %convolution_add_fusion.2), channel_id=1, source_target_pairs={{0,1},{1,2},{2,3},{3,4},{4,5},{5,6},{6,7},{8,9},{9,10},{10,11},{11... | collective-permute-start | bytes 1572872 | tf_op jit(solution)/shard_map/while/body/eval_jaxpr/ppermute | solution.py:25
  113.2 10.8 %collective-permute-start = (f32[8,128,128]{2,1,0:T(8,128)S(1)}, f32[8,128,128]{2,1,0:T(8,128)S(1)}, u32[]{:S(2)}, u32[]{:S(2)}) collective-permute-start(f32[8,128,128]{2,1,0:T(8,128)S(1)} %convolution_add_fusion.2), channel_id=1, source_target_pairs={{0,1},{1,2},{2,3},{3,4},{4,5},{5,6},{6,7},{8,9},{9,10},{10,11},{11... | collective-permute-start | bytes 1572872 | tf_op jit(solution)/shard_map/while/body/eval_jaxpr/ppermute | solution.py:25
  124.7 11.8 %collective-permute-start = (f32[8,128,128]{2,1,0:T(8,128)S(1)}, f32[8,128,128]{2,1,0:T(8,128)S(1)}, u32[]{:S(2)}, u32[]{:S(2)}) collective-permute-start(f32[8,128,128]{2,1,0:T(8,128)S(1)} %convolution_add_fusion.2), channel_id=1, source_target_pairs={{0,1},{1,2},{2,3},{3,4},{4,5},{5,6},{6,7},{8,9},{9,10},{10,11},{11... | collective-permute-start | bytes 1572872 | tf_op jit(solution)/shard_map/while/body/eval_jaxpr/ppermute | solution.py:25
  136.5 2.5 %copy-start.10 = (f32[256,1024]{0,1:T(8,128)S(1)}, f32[256,1024]{0,1:T(8,128)}, u32[]{:S(2)}) copy-start(f32[256,1024]{0,1:T(8,128)} %copy.17) | copy-start | bytes 3145732
  136.6 3.0 %copy-start.12 = (bf16[1024,2048]{1,0:T(8,128)(2,1)S(1)}, bf16[1024,2048]{1,0:T(8,128)(2,1)}, u32[]{:S(2)}) copy-start(bf16[1024,2048]{1,0:T(8,128)(2,1)} %param.27) | copy-start | bytes 12582916
Sparse Core Ops, SparseCore 0:
  142.3 41.9 reduce-scatter.1
where the time goes:
time: 196 us; the launch traced here: 193 us
  waiting for transfers between devices  118 us (60%)
  Pallas kernels  25.3 us (13%)
  local copies, waits for them, and re-layouts  13.5 us (7%)
  between operations  13.5 us (7%)
  starting transfers between devices  10.3 us (5%)
  matrix products  9.65 us (5%)
  other arithmetic  2.23 us (1%)
    ppermute x8, waiting for transfers between devices, shifted(): return lax.ppermute(block, axis, route)  76.1 us
    reduce_scatter x1, waiting for transfers between devices, local(): lax.psum_scatter(partial_sum, 'head', scatter_dimension=1, tiled=True)  42.1 us
    pallas_call x1, Pallas kernels, local(): pl.pallas_call(k1_body, grid=(khl,), in_specs=[pl.BlockSpec((n, DK), lamb...  25.3 us
    ppermute x8, starting transfers between devices, shifted(): return lax.ppermute(block, axis, route)  10.3 us
    unnamed x26, local copies, waits for them, and re-layouts  7.77 us
    dot_general x7, matrix products, matmul_hi(): jnp.einsum('...ij,...jk->...ik', left, right, precision=lax.Precision.HIG...  4.52 us
  transfers between devices with their start and end apart: 9, of which 9 were waited for; matrix products, arithmetic and copies ran while one was open for 1% of the time, Pallas kernels for 0%

commit v1 on v0

--- a/solution.py
+++ b/solution.py
@@ -120,7 +120,7 @@
 
 
 def k1_body(q_ref, k_ref, v_ref, hq_ref, hk_ref, hv_ref, cq_ref, ck_ref, cv_ref, a_ref, b_ref,
-            alog_ref, dt_ref, qe_ref, o_ref, m_ref, bb_ref, ext):
+            alog_ref, dt_ref, qe_ref, o_ref, d_ref, g_ref, bb_ref, ext):
     g = pl.program_id(0)
     n = q_ref.shape[0]
     q = unit(conv(q_ref[...], hq_ref[...], cq_ref[...], ext)) * DK ** (-0.5)
@@ -131,25 +131,122 @@
     alog2 = jnp.concatenate([jnp.full((1, n), alog_ref[g * RATIO + r], F32) for r in range(RATIO)], axis=0)
     dt2 = jnp.concatenate([jnp.full((1, n), dt_ref[g * RATIO + r], F32) for r in range(RATIO)], axis=0)
     terms = local_terms(q, k, v, a2, b2, alog2, dt2)
-    eye = jnp.where(
-        lax.broadcasted_iota(jnp.int32, (DK, DK), 0) == lax.broadcasted_iota(jnp.int32, (DK, DK), 1), 1.0, 0.0
-    )
     for r, (qe, o, d, bb, gl) in enumerate(terms):
         qe_ref[:, r * DV : (r + 1) * DV] = qe
         o_ref[:, r * DV : (r + 1) * DV] = o
-        m_ref[r] = gl * eye - d
+        d_ref[r] = d.astype(BF16)
+        g_ref[r] = jnp.broadcast_to(gl, (8, DV))
         bb_ref[r] = bb
 
 
-def matmul_hi(left, right):
-    return jnp.einsum("...ij,...jk->...ik", left, right, precision=lax.Precision.HIGHEST)
-
-
-def gated_norm(core, gate_in, norm_gain):
-    scale_rows = lax.rsqrt(jnp.mean(core * core, axis=-1, keepdims=True) + 1e-06)
-    gate_vals = gate_in.astype(F32).reshape(core.shape)
-    normalized_rows = core * scale_rows * norm_gain * jax.nn.silu(gate_vals)
-    return normalized_rows.astype(BF16).reshape(core.shape[0], -1)
+MESH = pl.DeviceIdType.MESH
+
+
+def k2_body(nh, nc, qe_ref, o_ref, d_ref, g_ref, bb_ref, gate_ref, gain_ref, w_hbm, out_ref,
+            gated, w, s_in, s_out, own, p1, r1, p2, r2, w_sem, s_send, s_recv, p1_send, p1_recv, p2_send, p2_recv):
+    head = lax.axis_index("head")
+    ctx = lax.axis_index("ctx")
+    nx = nh // 2
+    x = head // 2
+    core = head % 2
+    mate = x * 2 + (1 - core)
+    vhl = bb_ref.shape[0]
+    width = out_ref.shape[1]
+    peers = [((x + 1 + i) % nx) for i in range(nx)]
+
+    barrier = pltpu.get_barrier_semaphore()
+    pl.semaphore_signal(barrier, inc=1, device_id=(mate, ctx), device_id_type=MESH)
+    for i in range(nx - 1):
+        pl.semaphore_signal(barrier, inc=1, device_id=(peers[i] * 2 + core, ctx), device_id_type=MESH)
+
+    @pl.when(ctx > 0)
+    def _():
+        pl.semaphore_signal(barrier, inc=1, device_id=(head, ctx - 1), device_id_type=MESH)
+
+    @pl.when(ctx < nc - 1)
+    def _():
+        pl.semaphore_signal(barrier, inc=1, device_id=(head, ctx + 1), device_id_type=MESH)
+
+    w_copy = pltpu.make_async_copy(w_hbm, w, w_sem)
+    w_copy.start()
+    neighbours = jnp.minimum(ctx, 1) + jnp.minimum(nc - 1 - ctx, 1)
+    pl.semaphore_wait(barrier, nx + neighbours)
+
+    @pl.when(ctx == 0)
+    def _():
+        s_in[...] = jnp.zeros_like(s_in)
+
+    def state_copy(h):
+        return pltpu.make_async_remote_copy(
+            src_ref=s_out.at[h], dst_ref=s_in.at[h], send_sem=s_send.at[h], recv_sem=s_recv.at[h],
+            device_id=(head, ctx + 1), device_id_type=MESH,
+        )
+
+    def one_head(h, carry):
+        @pl.when(ctx > 0)
+        def _():
+            state_copy(h).wait_recv()
+
+        state = s_in[h]
+
+        @pl.when(ctx < nc - 1)
+        def _():
+            moved = g_ref[h][0:1, :] * state.astype(F32) - mm1(d_ref[h], state) + bb_ref[h]
+            s_out[h] = moved.astype(BF16)
+            state_copy(h).start()
+
+        columns = pl.ds(pl.multiple_of(h * DV, DV), DV)
+        qh, ql = split(qe_ref[:, columns])
+        values = o_ref[:, columns] + (mm1(qh, state) + mm1(ql, state))
+        scale = lax.rsqrt(jnp.mean(values * values, axis=-1, keepdims=True) + 1e-06)
+        gated[:, columns] = (values * scale * gain_ref[...] * silu(gate_ref[:, columns].astype(F32))).astype(BF16)
+        return carry
+
+    lax.fori_loop(0, vhl, one_head, 0)
+    w_copy.wait()
+
+    def block(index):
+        return mm1(gated[...], w[:, pl.ds(pl.multiple_of(index * width, 128), width)])
+
+    def mate_copy(i):
+        return pltpu.make_async_remote_copy(
+            src_ref=p1.at[i], dst_ref=r1.at[i], send_sem=p1_send.at[i], recv_sem=p1_recv.at[i],
+            device_id=(mate, ctx), device_id_type=MESH,
+        )
+
+    def chip_copy(i):
+        return pltpu.make_async_remote_copy(
+            src_ref=p2.at[i], dst_ref=r2.at[i], send_sem=p2_send.at[i], recv_sem=p2_recv.at[i],
+            device_id=(peers[i] * 2 + core, ctx), device_id_type=MESH,
+        )
+
+    for i in range(nx):
+        p1[i] = block(peers[i] * 2 + (1 - core)).astype(BF16)
+        mate_copy(i).start()
+    for i in range(nx - 1):
+        own[...] = block(peers[i] * 2 + core)
+        mate_copy(i).wait_recv()
+        p2[i] = (own[...] + r1[i].astype(F32)).astype(BF16)
+        chip_copy(i).start()
+    own[...] = block(head)
+    mate_copy(nx - 1).wait_recv()
+    total = own[...] + r1[nx - 1].astype(F32)
+    for i in range(nx - 1):
+        chip_copy(i).wait_recv()
+        total = total + r2[i].astype(F32)
+    out_ref[...] = total.astype(BF16)
+    for i in range(nx):
+        mate_copy(i).wait_send()
+    for i in range(nx - 1):
+        chip_copy(i).wait_send()
+
+    @pl.when(ctx < nc - 1)
+    def _():
+        def drain(h, carry):
+            state_copy(h).wait_send()
+            return carry
+
+        lax.fori_loop(0, vhl, drain, 0)
 
 
 def local(q_in, k_in, v_in, gate_in, conv_q, conv_k, value_conv_taps, a_in, b_in, a_log, dt_bias,
@@ -161,7 +258,7 @@
     before = shifted(tails, "ctx", 1)
     vw = RATIO * DV
     smem = pl.BlockSpec(memory_space=pltpu.SMEM)
-    qe, o, m, bb = pl.pallas_call(
+    qe, o, d, g_last, bb = pl.pallas_call(
         k1_body,
         grid=(khl,),
         in_specs=[
@@ -183,27 +280,54 @@
             pl.BlockSpec((n, vw), lambda g: (0, g)),
             pl.BlockSpec((n, vw), lambda g: (0, g)),
             pl.BlockSpec((RATIO, DK, DK), lambda g: (g, 0, 0)),
+            pl.BlockSpec((RATIO, 8, DV), lambda g: (g, 0, 0)),
             pl.BlockSpec((RATIO, DK, DV), lambda g: (g, 0, 0)),
         ],
         out_shape=[
             jax.ShapeDtypeStruct((n, vhl * DV), F32),
             jax.ShapeDtypeStruct((n, vhl * DV), F32),
-            jax.ShapeDtypeStruct((vhl, DK, DK), F32),
+            jax.ShapeDtypeStruct((vhl, DK, DK), BF16),
+            jax.ShapeDtypeStruct((vhl, 8, DV), F32),
             jax.ShapeDtypeStruct((vhl, DK, DV), F32),
         ],
         scratch_shapes=[pltpu.VMEM((n + 8, vw), F32)],
         compiler_params=pltpu.CompilerParams(vmem_limit_bytes=40 << 20),
     )(q_in, k_in, v_in, before, before, before, conv_q, conv_k, value_conv_taps, a_in, b_in, a_log, dt_bias)
 
-    def relay(index_now, incoming):
-        return shifted(matmul_hi(m, incoming) + bb, "ctx", 1)
-
-    start = lax.fori_loop(0, lax.axis_size("ctx") - 1, relay, jnp.zeros((vhl, DK, DV), F32))
-    core = jnp.einsum("thd,hde->the", qe.reshape(n, vhl, DK), start, precision=lax.Precision.HIGHEST)
-    core = core + o.reshape(n, vhl, DV)
-    gated = gated_norm(core, gate_in, norm_gain)
-    partial_sum = jnp.dot(gated, out_weight, preferred_element_type=F32)
-    return lax.psum_scatter(partial_sum, "head", scatter_dimension=1, tiled=True).astype(BF16)
+    nh = lax.axis_size("head")
+    nc = lax.axis_size("ctx")
+    nx = nh // 2
+    rows, total_width = out_weight.shape
+    width = total_width // nh
+    vmem = pl.BlockSpec(memory_space=pltpu.VMEM)
+    dma = pltpu.SemaphoreType.DMA
+    return pl.pallas_call(
+        functools.partial(k2_body, nh, nc),
+        in_specs=[vmem] * 7 + [pl.BlockSpec(memory_space=pl.ANY)],
+        out_specs=vmem,
+        out_shape=jax.ShapeDtypeStruct((n, width), BF16),
+        scratch_shapes=[
+            pltpu.VMEM((n, vhl * DV), BF16),
+            pltpu.VMEM((rows, total_width), BF16),
+            pltpu.VMEM((vhl, DK, DV), BF16),
+            pltpu.VMEM((vhl, DK, DV), BF16),
+            pltpu.VMEM((n, width), F32),
+            pltpu.VMEM((nx, n, width), BF16),
+            pltpu.VMEM((nx, n, width), BF16),
+            pltpu.VMEM((nx - 1, n, width), BF16),
+            pltpu.VMEM((nx - 1, n, width), BF16),
+            dma,
+            dma((vhl,)),
+            dma((vhl,)),
+            dma((nx,)),
+            dma((nx,)),
+            dma((nx - 1,)),
+            dma((nx - 1,)),
+        ],
+        compiler_params=pltpu.CompilerParams(
+            collective_id=0, has_side_effects=True, vmem_limit_bytes=40 << 20
+        ),
+    )(qe, o, d, g_last, bb, gate_in, norm_gain.reshape(1, DV), out_weight)
 
 
 def solution(mesh):

time: 196 us -> 82.6 us (0.42); the launches traced: 193 us -> 81.8 us
  waiting for transfers between devices: 118 us -> 3.18 us
  Pallas kernels: 25.3 us -> 62.8 us
  between operations: 13.5 us -> 0.05 us
  matrix products: 9.65 us -> 0 us
  starting transfers between devices: 10.3 us -> 1.29 us
  other arithmetic: 2.23 us -> 0.01 us
    ppermute x8 -> x1, waiting for transfers between devices: 76.1 us -> 3.18 us  [shifted(): return lax.ppermute(block, axis, route)]
    reduce_scatter x1 -> x0, waiting for transfers between devices: 42.1 us -> none  [local(): lax.psum_scatter(partial_sum, 'head', scatter_dimension=1, tiled=True)]
    pallas_call x0 -> x1, Pallas kernels: none -> 37.5 us  [local(): pl.pallas_call(functools.partial(k2_body, nh, nc), in_specs=[vmem] * 7 +...]
    dot_general x9 -> x0, matrix products: 9.65 us -> none  [the longest x7 4.52 us: matmul_hi(): jnp.einsum('...ij,...jk->...ik', left, right, precision=lax.Precision.HIG...]
    ppermute x8 -> x1, starting transfers between devices: 10.3 us -> 1.29 us  [shifted(): return lax.ppermute(block, axis, route)]
    unnamed x26 -> x27, local copies, waits for them, and re-layouts: 7.77 us -> 12.3 us
    reshape x2 -> x0, local copies, waits for them, and re-layouts: 3.56 us -> none  [the longest x1 2.23 us: gated_norm(): gate_vals = gate_in.astype(F32).reshape(core.shape)]
    convert_element_type x2 -> x0, other arithmetic: 2.21 us -> none  [the longest x1 1.77 us: local(): lax.psum_scatter(partial_sum, 'head', scatter_dimension=1, tiled=True)]
  transfers between devices with their start and end apart: 9 -> 1, of which waited for: 9 -> 1; matrix products, arithmetic and copies ran while one was open for 1% -> 0% of each run, Pallas kernels for 0% -> 0%
where the time goes in v1:
time: 82.6 us; the launch traced here: 81.8 us
  Pallas kernels  62.8 us (76%)
  local copies, waits for them, and re-layouts  14.5 us (18%)
  waiting for transfers between devices  3.18 us (4%)
  starting transfers between devices  1.29 us (2%)
    pallas_call x1, Pallas kernels, local(): pl.pallas_call(functools.partial(k2_body, nh, nc), in_specs=[vmem] * 7 +...  37.5 us
    pallas_call x1, Pallas kernels, local(): pl.pallas_call(k1_body, grid=(khl,), in_specs=[pl.BlockSpec((n, DK), lamb...  25.3 us
    unnamed x27, local copies, waits for them, and re-layouts  12.3 us
    ppermute x1, waiting for transfers between devices, shifted(): return lax.ppermute(block, axis, route)  3.18 us
    slice x3, local copies, waits for them, and re-layouts, local(): tails = jnp.concatenate([q_in[n - 3:], k_in[n - 3:], v_in[n - 3:]], axis=1)  2.13 us
  transfers between devices with their start and end apart: 1, of which 1 were waited for; matrix products, arithmetic and copies ran while one was open for 0% of the time, Pallas kernels for 0%

profile of v1, /device:TPU:29, one launch (start us, length us, event | category | flops | bytes accessed | tf_op | source)
XLA Modules:
  0.0 81.8 jit_solution(3597147506945038904)
XLA Ops:
  0.0 0.7 slice.9
  0.7 0.7 slice.10
  1.4 0.7 slice.11
  2.1 1.3 %collective-permute-start = (bf16[3,2048]{1,0:T(4,128)(2,1)S(1)}, bf16[3,2048]{1,0:T(4,128)(2,1)S(1)}, u32[]{:S(2)}, u32[]{:S(2)}) collective-permute-start(bf16[3,2048]{1,0:T(4,128)(2,1)S(1)} %pad_maximum_fusion), channel_id=1, source_target_pairs={{0,1},{1,2},{2,3},{3,4},{4,5},{5,6},{6,7},{8,9},{9,10},{10,11},{11... | collective-permute-start | bytes 36872 | tf_op jit(solution)/shard_map/ppermute | solution.py:25
  3.4 3.2 %collective-permute-done.hq_ref.hk_ref.hv_ref = bf16[3,2048]{1,0:T(4,128)(2,1)S(1)} collective-permute-done((bf16[3,2048]{1,0:T(4,128)(2,1)S(1)}, bf16[3,2048]{1,0:T(4,128)(2,1)S(1)}, u32[]{:S(2)}, u32[]{:S(2)}) %collective-permute-start) | collective-permute-done | bytes 12320 | tf_op jit(solution)/shard_map/ppermute | solution.py:25
  6.6 0.0 copy-start.1
  6.6 1.0 %copy-done.1 = bf16[256,1024]{1,0:T(8,128)(2,1)S(1)} copy-done((bf16[256,1024]{1,0:T(8,128)(2,1)S(1)}, bf16[256,1024]{1,0:T(8,128)(2,1)}, u32[]{:S(2)}) %copy-start.1) | copy-done | bytes 524312
  7.7 0.0 copy-start.3
  7.7 0.9 %copy-done.3 = bf16[256,512]{1,0:T(8,128)(2,1)S(1)} copy-done((bf16[256,512]{1,0:T(8,128)(2,1)S(1)}, bf16[256,512]{1,0:T(8,128)(2,1)}, u32[]{:S(2)}) %copy-start.3) | copy-done | bytes 262168
  8.6 0.0 copy-start.4
  8.6 0.9 %copy-done.4 = bf16[256,512]{1,0:T(8,128)(2,1)S(1)} copy-done((bf16[256,512]{1,0:T(8,128)(2,1)S(1)}, bf16[256,512]{1,0:T(8,128)(2,1)}, u32[]{:S(2)}) %copy-start.4) | copy-done | bytes 262168
  9.6 0.7 copy-done.5
  10.3 0.0 copy-start.6
  10.3 0.7 copy-done.6
  11.0 0.0 copy-start.7
  11.0 0.7 copy-done.7
  11.7 0.0 copy-start.8
  11.7 0.7 copy-done.8
  12.4 0.7 copy-done.9
  13.1 0.0 copy-start.10
  13.1 0.7 copy-done.10
  13.7 0.0 copy-start.11
  13.7 0.7 copy-done.11
  14.4 25.3 %shard_map.127 = (f32[256,1024]{1,0:T(8,128)S(1)}, f32[256,1024]{1,0:T(8,128)S(1)}, bf16[8,128,128]{2,1,0:T(8,128)(2,1)S(1)}, f32[8,8,128]{2,1,0:T(8,128)S(1)}, f32[8,128,128]{2,1,0:T(8,128)S(1)}) custom-call(bf16[256,512]{1,0:T(8,128)(2,1)S(1)} %copy-done.3, bf16[256,512]{1,0:T(8,128)(2,1)S(1)} %copy-done.4, bf16[256,1024]{1,0:T(8,128)(2,1)S(1)} %copy-done.1, ...), custom_call_target="tpu_custom_call" | custom-call | tf_op jit(solution)/shard_map/pallas_call | solution.py:261
  39.7 0.0 copy-start
  39.7 2.2 %copy-done = bf16[1024,2048]{1,0:T(8,128)(2,1)S(1)} copy-done((bf16[1024,2048]{1,0:T(8,128)(2,1)S(1)}, bf16[1024,2048]{1,0:T(8,128)(2,1)}, u32[]{:S(2)}) %copy-start) | copy-done | bytes 4194328
  41.9 0.0 copy-start.2
  41.9 1.0 %copy-done.2 = bf16[256,1024]{1,0:T(8,128)(2,1)S(1)} copy-done((bf16[256,1024]{1,0:T(8,128)(2,1)S(1)}, bf16[256,1024]{1,0:T(8,128)(2,1)}, u32[]{:S(2)}) %copy-start.2) | copy-done | bytes 524312
  43.0 0.0 copy-start.12
  43.0 0.7 copy-done.12
  43.6 37.5 %shard_map.128 = bf16[256,512]{1,0:T(8,128)(2,1)S(1)} custom-call(f32[256,1024]{1,0:T(8,128)S(1)} %get-tuple-element.10.qe_ref, f32[256,1024]{1,0:T(8,128)S(1)} %get-tuple-element.11.o_ref, bf16[8,128,128]{2,1,0:T(8,128)(2,1)S(1)} %get-tuple-element.12.d_ref, f32[8,8,128]{2,1,0:T(8,128)S(1)} %get-tuple-element.13.g_ref, ...), custom_call_target="tpu_custom_call" | custom-call | tf_op jit(solution)/shard_map/pallas_call | solution.py:304
  81.1 0.7 copy.15
  (3 shorter events, 0.0 us)
Async XLA Ops:
  2.1 4.5 %collective-permute-start = (bf16[3,2048]{1,0:T(4,128)(2,1)S(1)}, bf16[3,2048]{1,0:T(4,128)(2,1)S(1)}, u32[]{:S(2)}, u32[]{:S(2)}) collective-permute-start(bf16[3,2048]{1,0:T(4,128)(2,1)S(1)} %pad_maximum_fusion), channel_id=1, source_target_pairs={{0,1},{1,2},{2,3},{3,4},{4,5},{5,6},{6,7},{8,9},{9,10},{10,11},{11... | collective-permute-start | bytes 36872 | tf_op jit(solution)/shard_map/ppermute | solution.py:25
  6.6 1.0 %copy-start.1 = (bf16[256,1024]{1,0:T(8,128)(2,1)S(1)}, bf16[256,1024]{1,0:T(8,128)(2,1)}, u32[]{:S(2)}) copy-start(bf16[256,1024]{1,0:T(8,128)(2,1)} %v_ref.1) | copy-start | bytes 1572868
  7.7 0.9 %copy-start.3 = (bf16[256,512]{1,0:T(8,128)(2,1)S(1)}, bf16[256,512]{1,0:T(8,128)(2,1)}, u32[]{:S(2)}) copy-start(bf16[256,512]{1,0:T(8,128)(2,1)} %q_ref.1) | copy-start | bytes 786436
  8.6 0.9 %copy-start.4 = (bf16[256,512]{1,0:T(8,128)(2,1)S(1)}, bf16[256,512]{1,0:T(8,128)(2,1)}, u32[]{:S(2)}) copy-start(bf16[256,512]{1,0:T(8,128)(2,1)} %k_ref.1) | copy-start | bytes 786436
  9.6 0.7 copy-start.5
  10.3 0.7 copy-start.6
  11.0 0.7 copy-start.7
  11.7 0.7 copy-start.8
  12.4 0.7 copy-start.9
  13.1 0.7 copy-start.10
  13.7 0.7 copy-start.11
  39.7 2.2 %copy-start = (bf16[1024,2048]{1,0:T(8,128)(2,1)S(1)}, bf16[1024,2048]{1,0:T(8,128)(2,1)}, u32[]{:S(2)}) copy-start(bf16[1024,2048]{1,0:T(8,128)(2,1)} %w_hbm.1) | copy-start | bytes 12582916
  41.9 1.0 %copy-start.2 = (bf16[256,1024]{1,0:T(8,128)(2,1)S(1)}, bf16[256,1024]{1,0:T(8,128)(2,1)}, u32[]{:S(2)}) copy-start(bf16[256,1024]{1,0:T(8,128)(2,1)} %gate_ref.1) | copy-start | bytes 1572868
  43.0 0.7 copy-start.12

commit v2 on v1

v2 whole, which is shorter than its diff:
```python
import functools

import jax
import jax.numpy as jnp
from jax import lax
from jax.experimental import pallas as pl
from jax.experimental.pallas import tpu as pltpu
from jax.sharding import PartitionSpec as P

KH = 16
VH = 32
DK = 128
DV = 128
RATIO = VH // KH
SIDE = 128
F32 = jnp.float32
BF16 = jnp.bfloat16
NN = (((1,), (0,)), ((), ()))
NT = (((1,), (1,)), ((), ()))
TN = (((0,), (0,)), ((), ()))


def mm1(left, right, dims=NN):
    return lax.dot_general(left.astype(BF16), right.astype(BF16), dims, preferred_element_type=F32)


def split(x):
    high = x.astype(BF16)
    return high, (x - high.astype(F32)).astype(BF16)


def mm3(left, right, dims=NN):
    lh, ll = split(left)
    rh, rl = split(right)
    return mm1(lh, rh, dims) + (mm1(lh, rl, dims) + mm1(ll, rh, dims))


def exact_left(mask, right, dims):
    high, low = split(right)
    rest = (right - high.astype(F32) - low.astype(F32)).astype(BF16)
    return mm1(mask, high, dims) + (mm1(mask, low, dims) + mm1(mask, rest, dims))


def silu(x):
    return x / (1.0 + jnp.exp(-x))


def conv(x, halo, taps, ext):
    length, width = x.shape
    ext[0:8, :width] = halo.astype(F32)[8:16]
    ext[8 : 8 + length, :width] = x.astype(F32)
    total = taps[0:1] * ext[5 : 5 + length, :width]
    for j in range(1, 4):
        total = total + taps[j : j + 1] * ext[5 + j : 5 + j + length, :width]
    return silu(total)


def unit(x):
    return x * lax.rsqrt(jnp.sum(x * x, axis=-1, keepdims=True) + 1e-06)


def pick_row(x, h):
    index = lax.broadcasted_iota(jnp.int32, x.shape, 0)
    return jnp.sum(jnp.where(index == h, x, 0.0), axis=0, keepdims=True)


def local_terms(heads, ld, strength):
    n = heads[0][0].shape[0]
    nb = n // SIDE
    row = lax.broadcasted_iota(jnp.int32, (n, n), 0)
    col = lax.broadcasted_iota(jnp.int32, (n, n), 1)
    tri = jnp.where(row >= col, 1.0, 0.0).astype(BF16)
    diag = jnp.where(row == col, 1.0, 0.0).astype(BF16)
    l0, l1 = split(ld)
    l2 = (ld - l0.astype(F32) - l1.astype(F32)).astype(BF16)
    c_row = mm1(l0, tri, NT) + mm1(l1, tri, NT) + mm1(l2, tri, NT)
    c_col = exact_left(tri, ld, NT)
    b_col = exact_left(diag, strength, NT)
    brow = lax.broadcasted_iota(jnp.int32, (SIDE, SIDE), 0)
    bcol = lax.broadcasted_iota(jnp.int32, (SIDE, SIDE), 1)
    xor = jnp.where(brow > bcol, brow ^ bcol, 0)
    level = jnp.where(xor > 0, 0, -1)
    span = 2
    while span < SIDE:
        level = level + jnp.where(xor >= span, 1, 0)
        span *= 2
    lower = brow >= bcol
    eye = jnp.where(brow == bcol, 1.0, 0.0)

    def part(i):
        return slice(i * SIDE, (i + 1) * SIDE)

    items = []
    for g, (q, k, v) in enumerate(heads):
        kk = mm1(k, k, NT)
        qk = mm3(q, k, NT)
        for r in range(RATIO):
            h = g * RATIO + r
            cc = c_col[:, h : h + 1]
            bc = b_col[:, h : h + 1]
            low, scores = {}, {}
            for i in range(nb):
                for j in range(i + 1):
                    gap = jnp.minimum(cc[part(i)] - c_row[h : h + 1, part(j)], 0.0)
                    damp = jnp.exp(gap)
                    lo = bc[part(i)] * kk[part(i), part(j)] * damp
                    sc = qk[part(i), part(j)] * damp
                    if i == j:
                        lo = jnp.where(level >= 0, lo, 0.0)
                        sc = jnp.where(lower, sc, 0.0)
                    low[i, j] = lo
                    scores[i, j] = sc
            gate = jnp.exp(cc)
            rhs = jnp.concatenate([bc * gate * k, bc * v[:, r * DV : (r + 1) * DV]], axis=1)
            items.append((q, k, cc, gate, low, scores, rhs))

    blocks = [low[i, i] for (_, _, _, _, low, _, _) in items for i in range(nb)]
    inverses = [eye - jnp.where(level == 0, block, 0.0) for block in blocks]
    depth = 1
    while (1 << depth) < SIDE:
        held = [inv.astype(BF16) for inv in inverses]
        first = [mm1(hb, jnp.where(level == depth, block, 0.0)) for hb, block in zip(held, blocks)]
        inverses = [inv - mm1(p, hb) for inv, p, hb in zip(inverses, first, held)]
        depth += 1
    held = [inv.astype(BF16) for inv in inverses]

    solved = [[] for _ in items]
    for i in range(nb):
        targets = []
        for t, (_, _, _, _, low, _, rhs) in enumerate(items):
            target = rhs[part(i)]
            for j in range(i):
                target = target - mm1(low[i, j], solved[t][j])
            targets.append(target)
        guess = [mm1(held[t * nb + i], target) for t, target in enumerate(targets)]
        rest = [
            target - y - mm1(items[t][4][i, i], y) for t, (target, y) in enumerate(zip(targets, guess))
        ]
        for t in range(len(items)):
            solved[t].append(guess[t] + mm1(held[t * nb + i], rest[t]))

    results = []
    for t, (q, k, cc, gate, _, scores, _) in enumerate(items):
        y = jnp.concatenate(solved[t], axis=0)
        yh, yl = split(y)
        outs = []
        for i in range(nb):
            sc = jnp.concatenate([scores[i, j] for j in range(i + 1)], axis=1)
            sh, sl = split(sc)
            top = (i + 1) * SIDE
            outs.append(mm1(sh, yh[:top]) + (mm1(sh, yl[:top]) + mm1(sl, yh[:top])))
        sy = jnp.concatenate(outs, axis=0)
        last = cc[n - 1 : n]
        kh, kl = split(jnp.exp(last - cc) * k)
        ky = mm1(kh, yh, TN) + (mm1(kh, yl, TN) + mm1(kl, yh, TN))
        results.append((gate * q - sy[:, :DK], sy[:, DK:], ky[:, :DK], ky[:, DK:], jnp.exp(last)))
    return results


MESH = pl.DeviceIdType.MESH


def body(nh, nc, alog_ref, dt_ref, q_hbm, k_hbm, v_hbm, cq_hbm, ck_hbm, cv_hbm, a_hbm, b_hbm,
         gate_hbm, gain_hbm, w_hbm, out_ref,
         q_ref, k_ref, v_ref, cq_ref, ck_ref, cv_ref, a_ref, b_ref, gate_ref, gain_ref, w,
         hq, hk, hv, ext, qe_ref, o_ref, d_ref, g_ref, bb_ref,
         gated, s_in, s_out, own, p1, r1, p2, r2,
         in_sem, h_send, h_recv, s_send, s_recv, p1_send, p1_recv, p2_send, p2_recv):
    head = lax.axis_index("head")
    ctx = lax.axis_index("ctx")
    nx = nh // 2
    x = head // 2
    core = head % 2
    mate = x * 2 + (1 - core)
    n = q_ref.shape[0]
    khl = q_ref.shape[1] // DK
    vhl = khl * RATIO
    width = out_ref.shape[1]
    peers = [((x + 1 + i) % nx) for i in range(nx)]

    barrier = pltpu.get_barrier_semaphore()
    pl.semaphore_signal(barrier, inc=1, device_id=(mate, ctx), device_id_type=MESH)
    for i in range(nx - 1):
        pl.semaphore_signal(barrier, inc=1, device_id=(peers[i] * 2 + core, ctx), device_id_type=MESH)

    @pl.when(ctx > 0)
    def _():
        pl.semaphore_signal(barrier, inc=1, device_id=(head, ctx - 1), device_id_type=MESH)

    @pl.when(ctx < nc - 1)
    def _():
        pl.semaphore_signal(barrier, inc=1, device_id=(head, ctx + 1), device_id_type=MESH)

    pairs = [
        (q_hbm, q_ref), (k_hbm, k_ref), (v_hbm, v_ref), (cq_hbm, cq_ref), (ck_hbm, ck_ref), (cv_hbm, cv_ref),
        (a_hbm, a_ref), (b_hbm, b_ref), (gate_hbm, gate_ref), (gain_hbm, gain_ref), (w_hbm, w),
    ]
    loads = [pltpu.make_async_copy(src, dst, in_sem.at[i]) for i, (src, dst) in enumerate(pairs)]
    for load in loads:
        load.start()

    neighbours = jnp.minimum(ctx, 1) + jnp.minimum(nc - 1 - ctx, 1)
    pl.semaphore_wait(barrier, nx + neighbours)

    halos = [
        pltpu.make_async_remote_copy(
            src_ref=src.at[pl.ds(n - 16, 16)], dst_ref=dst, send_sem=h_send.at[i], recv_sem=h_recv.at[i],
            device_id=(head, ctx + 1), device_id_type=MESH,
        )
        for i, (src, dst) in enumerate([(q_hbm, hq), (k_hbm, hk), (v_hbm, hv)])
    ]

    @pl.when(ctx < nc - 1)
    def _():
        for halo in halos:
            halo.start()

    @pl.when(ctx == 0)
    def _():
        hq[...] = jnp.zeros_like(hq)
        hk[...] = jnp.zeros_like(hk)
        hv[...] = jnp.zeros_like(hv)
        s_in[...] = jnp.zeros_like(s_in)

    for load in loads[:8]:
        load.wait()

    @pl.when(ctx > 0)
    def _():
        for halo in halos:
            halo.wait_recv()

    group = 2 if khl % 2 == 0 else 1
    vw = RATIO * DV

    def local_step(step, carry):
        heads, lds, strengths = [], [], []
        for t in range(group):
            g = step * group + t
            kc = pl.ds(pl.multiple_of(g * DK, DK), DK)
            vc = pl.ds(pl.multiple_of(g * vw, vw), vw)
            q = unit(conv(q_ref[:, kc], hq[:, kc], cq_ref[:, kc], ext)) * DK ** (-0.5)
            k = unit(conv(k_ref[:, kc], hk[:, kc], ck_ref[:, kc], ext))
            v = conv(v_ref[:, vc], hv[:, vc], cv_ref[:, vc], ext)
            heads.append((q, k, v))
            for r in range(RATIO):
                h = g * RATIO + r
                ax = pick_row(a_ref[...], h) + dt_ref[h]
                rate = jnp.exp(jnp.full((1, n), alog_ref[h], F32))
                lds.append(-rate * (jnp.maximum(ax, 0.0) + jnp.log1p(jnp.exp(-jnp.abs(ax)))))
                strengths.append(1.0 / (1.0 + jnp.exp(-pick_row(b_ref[...], h))))
        terms = local_terms(heads, jnp.concatenate(lds, axis=0), jnp.concatenate(strengths, axis=0))
        for t, (qe, o, d, bb, gl) in enumerate(terms):
            h = step * (group * RATIO) + t
            columns = pl.ds(pl.multiple_of(h * DV, DV), DV)
            qe_ref[:, columns] = qe
            o_ref[:, columns] = o
            d_ref[h] = d.astype(BF16)
            g_ref[h] = jnp.broadcast_to(gl, (8, DV))
            bb_ref[h] = bb
        return carry

    lax.fori_loop(0, khl // group, local_step, 0)

    for load in loads[8:10]:
        load.wait()

    def state_copy(p):
        both = pl.ds(p * RATIO, RATIO)
        return pltpu.make_async_remote_copy(
            src_ref=s_out.at[both], dst_ref=s_in.at[both], send_sem=s_send.at[p], recv_sem=s_recv.at[p],
            device_id=(head, ctx + 1), device_id_type=MESH,
        )

    def one_pair(p, carry):
        @pl.when(ctx > 0)
        def _():
            state_copy(p).wait_recv()

        @pl.when(ctx < nc - 1)
        def _():
            for r in range(RATIO):
                h = p * RATIO + r
                state = s_in[h]
                moved = g_ref[h][0:1, :] * state.astype(F32) - mm1(d_ref[h], state) + bb_ref[h]
                s_out[h] = moved.astype(BF16)
            state_copy(p).start()

        for r in range(RATIO):
            h = p * RATIO + r
            state = s_in[h]
            columns = pl.ds(pl.multiple_of(h * DV, DV), DV)
            qh, ql = split(qe_ref[:, columns])
            values = o_ref[:, columns] + (mm1(qh, state) + mm1(ql, state))
            scale = lax.rsqrt(jnp.mean(values * values, axis=-1, keepdims=True) + 1e-06)
            gate = silu(gate_ref[:, columns].astype(F32))
            gated[:, columns] = (values * scale * gain_ref[...] * gate).astype(BF16)
        return carry

    lax.fori_loop(0, khl, one_pair, 0)
    loads[10].wait()

    def block(index):
        return mm1(gated[...], w[:, pl.ds(pl.multiple_of(index * width, 128), width)])

    def mate_copy(i):
        return pltpu.make_async_remote_copy(
            src_ref=p1.at[i], dst_ref=r1.at[i], send_sem=p1_send.at[i], recv_sem=p1_recv.at[i],
            device_id=(mate, ctx), device_id_type=MESH,
        )

    def chip_copy(i):
        return pltpu.make_async_remote_copy(
            src_ref=p2.at[i], dst_ref=r2.at[i], send_sem=p2_send.at[i], recv_sem=p2_recv.at[i],
            device_id=(peers[i] * 2 + core, ctx), device_id_type=MESH,
        )

    for i in range(nx):
        p1[i] = block(peers[i] * 2 + (1 - core)).astype(BF16)
        mate_copy(i).start()
    for i in range(nx - 1):
        own[...] = block(peers[i] * 2 + core)
        mate_copy(i).wait_recv()
        p2[i] = (own[...] + r1[i].astype(F32)).astype(BF16)
        chip_copy(i).start()
    own[...] = block(head)
    mate_copy(nx - 1).wait_recv()
    total = own[...] + r1[nx - 1].astype(F32)
    for i in range(nx - 1):
        chip_copy(i).wait_recv()
        total = total + r2[i].astype(F32)
    out_ref[...] = total.astype(BF16)
    for i in range(nx):
        mate_copy(i).wait_send()
    for i in range(nx - 1):
        chip_copy(i).wait_send()

    @pl.when(ctx < nc - 1)
    def _():
        def drain(h, carry):
            state_copy(h).wait_send()
            return carry

        lax.fori_loop(0, khl, drain, 0)
        for halo in halos:
            halo.wait_send()


def local(q_in, k_in, v_in, gate_in, conv_q, conv_k, value_conv_taps, a_in, b_in, a_log, dt_bias,
          norm_gain, out_weight):
    n = q_in.shape[0]
    khl = q_in.shape[1] // DK
    vhl = khl * RATIO
    nh = lax.axis_size("head")
    nc = lax.axis_size("ctx")
    nx = nh // 2
    rows, total_width = out_weight.shape
    width = total_width // nh
    smem = pl.BlockSpec(memory_space=pltpu.SMEM)
    hbm = pl.BlockSpec(memory_space=pltpu.HBM)
    dma = pltpu.SemaphoreType.DMA
    operands = (q_in, k_in, v_in, conv_q, conv_k, value_conv_taps, a_in, b_in, gate_in,
                norm_gain.reshape(1, DV), out_weight)
    vmem = pltpu.VMEM
    return pl.pallas_call(
        functools.partial(body, nh, nc),
        in_specs=[smem, smem] + [hbm] * len(operands),
        out_specs=pl.BlockSpec(memory_space=pltpu.VMEM),
        out_shape=jax.ShapeDtypeStruct((n, width), BF16),
        scratch_shapes=[vmem(op.shape, op.dtype) for op in operands] + [
            vmem((16, q_in.shape[1]), BF16),
            vmem((16, k_in.shape[1]), BF16),
            vmem((16, v_in.shape[1]), BF16),
            vmem((n + 8, RATIO * DV), F32),
            vmem((n, vhl * DK), F32),
            vmem((n, vhl * DV), F32),
            vmem((vhl, DK, DK), BF16),
            vmem((vhl, 8, DV), F32),
            vmem((vhl, DK, DV), F32),
            vmem((n, vhl * DV), BF16),
            vmem((vhl, DK, DV), BF16),
            vmem((vhl, DK, DV), BF16),
            vmem((n, width), F32),
            vmem((nx, n, width), BF16),
            vmem((nx, n, width), BF16),
            vmem((nx - 1, n, width), BF16),
            vmem((nx - 1, n, width), BF16),
            dma((len(operands),)),
            dma((3,)),
            dma((3,)),
            dma((khl,)),
            dma((khl,)),
            dma((nx,)),
            dma((nx,)),
            dma((nx - 1,)),
            dma((nx - 1,)),
        ],
        compiler_params=pltpu.CompilerParams(
            collective_id=0, has_side_effects=True, vmem_limit_bytes=63 << 20
        ),
    )(a_log, dt_bias, *operands)


def solution(mesh):
    return jax.shard_map(
        local,
        mesh=mesh,
        in_specs=(
            P("ctx", "head"),
            P("ctx", "head"),
            P("ctx", "head"),
            P("ctx", "head"),
            P(None, "head"),
            P(None, "head"),
            P(None, "head"),
            P("head", "ctx"),
            P("head", "ctx"),
            P("head"),
            P("head"),
            P(),
            P("head", None),
        ),
        out_specs=P("ctx", "head"),
        check_vma=False,
    )
```

time: 82.6 us -> 52.5 us (0.64)
  local copies, waits for them, and re-layouts: 14.5 us -> 1.67 us
  Pallas kernels: 62.8 us -> 50.7 us
  waiting for transfers between devices: 3.18 us -> 0 us
  starting transfers between devices: 1.29 us -> 0 us
    pallas_call x2 -> x1, Pallas kernels: 62.8 us -> 50.7 us  [local(): pl.pallas_call(functools.partial(body, nh, nc), in_specs=[smem, smem] + [...]
    unnamed x27 -> x1, local copies, waits for them, and re-layouts: 12.3 us -> 1.67 us
    ppermute x1 -> x0, waiting for transfers between devices: 3.18 us -> none  [shifted(): return lax.ppermute(block, axis, route)]
    slice x3 -> x0, local copies, waits for them, and re-layouts: 2.13 us -> none  [local(): tails = jnp.concatenate([q_in[n - 3:], k_in[n - 3:], v_in[n - 3:]], axis=1)]
    ppermute x1 -> x0, starting transfers between devices: 1.29 us -> none  [shifted(): return lax.ppermute(block, axis, route)]
  transfers between devices with their start and end apart: 1 -> 0, of which waited for: 1 -> 0; matrix products, arithmetic and copies ran while one was open for 0% -> 0% of each run, Pallas kernels for 0% -> 0%
where the time goes in v2:
time: 52.5 us; the launch traced here: 52.3 us
  Pallas kernels  50.7 us (97%)
  local copies, waits for them, and re-layouts  1.67 us (3%)
    pallas_call x1, Pallas kernels, local(): pl.pallas_call(functools.partial(body, nh, nc), in_specs=[smem, smem] + [...  50.7 us
    unnamed x1, local copies, waits for them, and re-layouts  1.67 us

profile of v2, /device:TPU:29, one launch (start us, length us, event | category | flops | bytes accessed | tf_op | source)
XLA Modules:
  0.0 52.3 jit_solution(18425910304619382279)
XLA Ops:
  0.0 50.7 %shard_map.127 = bf16[256,512]{1,0:T(8,128)(2,1)} custom-call(f32[8]{0:T(128)} %alog_ref.1, f32[8]{0:T(128)} %dt_ref.1, bf16[256,512]{1,0:T(8,128)(2,1)} %q_hbm.1, bf16[256,512]{1,0:T(8,128)(2,1)} %k_hbm.1, bf16[256,1024]{1,0:T(8,128)(2,1)} %v_hbm.1, f32[4,512]{1,0:T(4,128)} %cq_hbm.1, f32[4,512]{1,0:T(4,128)} %ck_hbm.1, f32[4,1024]{1,0:T(4,128)} %cv_hbm.1, ...), custom_call_target="tpu_custom_call" | custom-call | tf_op jit(solution)/shard_map/pallas_call | solution.py:365
  50.7 1.7 %copy.15 = bf16[256,512]{1,0:T(8,128)(2,1)} copy(bf16[256,512]{1,0:T(8,128)(2,1)} %shard_map.127) | data formatting | bytes 524288

commit v3 on v2

--- a/solution.py
+++ b/solution.py
@@ -146,13 +146,12 @@
         outs = []
         for i in range(nb):
             sc = jnp.concatenate([scores[i, j] for j in range(i + 1)], axis=1)
-            sh, sl = split(sc)
             top = (i + 1) * SIDE
-            outs.append(mm1(sh, yh[:top]) + (mm1(sh, yl[:top]) + mm1(sl, yh[:top])))
+            outs.append(mm1(sc, yh[:top]) + mm1(sc, yl[:top]))
         sy = jnp.concatenate(outs, axis=0)
         last = cc[n - 1 : n]
-        kh, kl = split(jnp.exp(last - cc) * k)
-        ky = mm1(kh, yh, TN) + (mm1(kh, yl, TN) + mm1(kl, yh, TN))
+        kh = (jnp.exp(last - cc) * k).astype(BF16)
+        ky = mm1(kh, yh, TN) + mm1(kh, yl, TN)
         results.append((gate * q - sy[:, :DK], sy[:, DK:], ky[:, :DK], ky[:, DK:], jnp.exp(last)))
     return results
 
@@ -164,7 +163,7 @@
          gate_hbm, gain_hbm, w_hbm, out_ref,
          q_ref, k_ref, v_ref, cq_ref, ck_ref, cv_ref, a_ref, b_ref, gate_ref, gain_ref, w,
          hq, hk, hv, ext, qe_ref, o_ref, d_ref, g_ref, bb_ref,
-         gated, s_in, s_out, own, p1, r1, p2, r2,
+         gated, acc, s_in, s_out, own, p1, r1, p2, r2,
          in_sem, h_send, h_recv, s_send, s_recv, p1_send, p1_recv, p2_send, p2_recv):
     head = lax.axis_index("head")
     ctx = lax.axis_index("ctx")
@@ -265,43 +264,60 @@
     for load in loads[8:10]:
         load.wait()
 
-    def state_copy(p):
-        both = pl.ds(p * RATIO, RATIO)
+    def state_copy(h):
         return pltpu.make_async_remote_copy(
-            src_ref=s_out.at[both], dst_ref=s_in.at[both], send_sem=s_send.at[p], recv_sem=s_recv.at[p],
+            src_ref=s_out.at[h], dst_ref=s_in.at[h], send_sem=s_send.at[h], recv_sem=s_recv.at[h],
             device_id=(head, ctx + 1), device_id_type=MESH,
         )
 
-    def one_pair(p, carry):
-        @pl.when(ctx > 0)
-        def _():
-            state_copy(p).wait_recv()
-
-        @pl.when(ctx < nc - 1)
+    @pl.when(ctx < nc - 1)
+    def _():
+        def relay(h, carry):
+            @pl.when(ctx > 0)
+            def _():
+                state_copy(h).wait_recv()
+
+            state = s_in[h]
+            moved = (g_ref[h][0:1, :] * state.astype(F32) + bb_ref[h]) - mm1(d_ref[h], state)
+            s_out[h] = moved.astype(BF16)
+            state_copy(h).start()
+            return carry
+
+        lax.fori_loop(0, vhl, relay, 0)
+
+    loads[10].wait()
+
+    def finish_pair(p):
+        @pl.when(ctx == nc - 1)
         def _():
             for r in range(RATIO):
-                h = p * RATIO + r
-                state = s_in[h]
-                moved = g_ref[h][0:1, :] * state.astype(F32) - mm1(d_ref[h], state) + bb_ref[h]
-                s_out[h] = moved.astype(BF16)
-            state_copy(p).start()
+                state_copy(p * RATIO + r).wait_recv()
 
         for r in range(RATIO):
             h = p * RATIO + r
             state = s_in[h]
-            columns = pl.ds(pl.multiple_of(h * DV, DV), DV)
+            columns = pl.ds(h * DV if isinstance(h, int) else pl.multiple_of(h * DV, DV), DV)
             qh, ql = split(qe_ref[:, columns])
             values = o_ref[:, columns] + (mm1(qh, state) + mm1(ql, state))
             scale = lax.rsqrt(jnp.mean(values * values, axis=-1, keepdims=True) + 1e-06)
             gate = silu(gate_ref[:, columns].astype(F32))
-            gated[:, columns] = (values * scale * gain_ref[...] * gate).astype(BF16)
+            gated[:, r * DV : (r + 1) * DV] = (values * scale * gain_ref[...] * gate).astype(BF16)
+
+    def add_pair(p, carry):
+        finish_pair(p)
+        rows = pl.ds(pl.multiple_of(p * vw, vw), vw)
+        for j in range(nh):
+            cols = slice(j * width, (j + 1) * width)
+            acc[:, cols] = acc[:, cols] + mm1(gated[...], w[rows, cols])
         return carry
 
-    lax.fori_loop(0, khl, one_pair, 0)
-    loads[10].wait()
+    acc[...] = jnp.zeros_like(acc)
+    lax.fori_loop(0, khl - 1, add_pair, 0)
+    finish_pair(khl - 1)
 
     def block(index):
-        return mm1(gated[...], w[:, pl.ds(pl.multiple_of(index * width, 128), width)])
+        cols = pl.ds(pl.multiple_of(index * width, 128), width)
+        return acc[:, cols] + mm1(gated[...], w[pl.ds((khl - 1) * vw, vw), cols])
 
     def mate_copy(i):
         return pltpu.make_async_remote_copy(
@@ -341,7 +357,7 @@
             state_copy(h).wait_send()
             return carry
 
-        lax.fori_loop(0, khl, drain, 0)
+        lax.fori_loop(0, vhl, drain, 0)
         for halo in halos:
             halo.wait_send()
 
@@ -377,7 +393,8 @@
             vmem((vhl, DK, DK), BF16),
             vmem((vhl, 8, DV), F32),
             vmem((vhl, DK, DV), F32),
-            vmem((n, vhl * DV), BF16),
+            vmem((n, RATIO * DV), BF16),
+            vmem((n, total_width), F32),
             vmem((vhl, DK, DV), BF16),
             vmem((vhl, DK, DV), BF16),
             vmem((n, width), F32),
@@ -388,8 +405,8 @@
             dma((len(operands),)),
             dma((3,)),
             dma((3,)),
-            dma((khl,)),
-            dma((khl,)),
+            dma((vhl,)),
+            dma((vhl,)),
             dma((nx,)),
             dma((nx,)),
             dma((nx - 1,)),

time: 52.5 us -> 48.6 us (0.926)
  Pallas kernels: 50.7 us -> 46.8 us
    pallas_call x1, Pallas kernels: 50.7 us -> 46.8 us  [local(): pl.pallas_call(functools.partial(body, nh, nc), in_specs=[smem, smem] + [...]
where the time goes in v3:
time: 48.6 us; the launch traced here: 48.4 us
  Pallas kernels  46.8 us (96%)
  local copies, waits for them, and re-layouts  1.67 us (3%)
    pallas_call x1, Pallas kernels, local(): pl.pallas_call(functools.partial(body, nh, nc), in_specs=[smem, smem] + [...  46.8 us
    unnamed x1, local copies, waits for them, and re-layouts  1.67 us

profile of v3, /device:TPU:29, one launch (start us, length us, event | category | flops | bytes accessed | tf_op | source)
XLA Modules:
  0.0 48.4 jit_solution(9581977897432033272)
XLA Ops:
  0.0 46.8 %shard_map.127 = bf16[256,512]{1,0:T(8,128)(2,1)} custom-call(f32[8]{0:T(128)} %alog_ref.1, f32[8]{0:T(128)} %dt_ref.1, bf16[256,512]{1,0:T(8,128)(2,1)} %q_hbm.1, bf16[256,512]{1,0:T(8,128)(2,1)} %k_hbm.1, bf16[256,1024]{1,0:T(8,128)(2,1)} %v_hbm.1, f32[4,512]{1,0:T(4,128)} %cq_hbm.1, f32[4,512]{1,0:T(4,128)} %ck_hbm.1, f32[4,1024]{1,0:T(4,128)} %cv_hbm.1, ...), custom_call_target="tpu_custom_call" | custom-call | tf_op jit(solution)/shard_map/pallas_call | solution.py:381
  46.8 1.7 %copy.15 = bf16[256,512]{1,0:T(8,128)(2,1)} copy(bf16[256,512]{1,0:T(8,128)(2,1)} %shard_map.127) | data formatting | bytes 524288

commit v4 on v3

--- a/solution.py
+++ b/solution.py
@@ -163,8 +163,8 @@
          gate_hbm, gain_hbm, w_hbm, out_ref,
          q_ref, k_ref, v_ref, cq_ref, ck_ref, cv_ref, a_ref, b_ref, gate_ref, gain_ref, w,
          hq, hk, hv, ext, qe_ref, o_ref, d_ref, g_ref, bb_ref,
-         gated, acc, s_in, s_out, own, p1, r1, p2, r2,
-         in_sem, h_send, h_recv, s_send, s_recv, p1_send, p1_recv, p2_send, p2_recv):
+         gated, acc, s_in, s_out, f_out, db, pdb, pg, own, p1, r1, p2, r2,
+         in_sem, h_send, h_recv, s_send, s_recv, f_send, f_recv, e_send, e_recv, p1_send, p1_recv, p2_send, p2_recv):
     head = lax.axis_index("head")
     ctx = lax.axis_index("ctx")
     nx = nh // 2
@@ -190,6 +190,16 @@
     def _():
         pl.semaphore_signal(barrier, inc=1, device_id=(head, ctx + 1), device_id_type=MESH)
 
+    even = ctx % 2 == 0
+
+    @pl.when(jnp.logical_and(even, ctx > 1))
+    def _():
+        pl.semaphore_signal(barrier, inc=1, device_id=(head, ctx - 2), device_id_type=MESH)
+
+    @pl.when(jnp.logical_and(even, ctx < nc - 2))
+    def _():
+        pl.semaphore_signal(barrier, inc=1, device_id=(head, ctx + 2), device_id_type=MESH)
+
     pairs = [
         (q_hbm, q_ref), (k_hbm, k_ref), (v_hbm, v_ref), (cq_hbm, cq_ref), (ck_hbm, ck_ref), (cv_hbm, cv_ref),
         (a_hbm, a_ref), (b_hbm, b_ref), (gate_hbm, gate_ref), (gain_hbm, gain_ref), (w_hbm, w),
@@ -199,7 +209,8 @@
         load.start()
 
     neighbours = jnp.minimum(ctx, 1) + jnp.minimum(nc - 1 - ctx, 1)
-    pl.semaphore_wait(barrier, nx + neighbours)
+    seconds = (1 - ctx % 2) * (jnp.minimum(ctx // 2, 1) + jnp.minimum((nc - 1 - ctx) // 2, 1))
+    pl.semaphore_wait(barrier, nx + neighbours + seconds)
 
     halos = [
         pltpu.make_async_remote_copy(
@@ -231,6 +242,21 @@
 
     group = 2 if khl % 2 == 0 else 1
     vw = RATIO * DV
+
+    per_step = group * RATIO
+
+    def pair_copies(step):
+        some = pl.ds(step * per_step, per_step)
+        return [
+            pltpu.make_async_remote_copy(
+                src_ref=src.at[some], dst_ref=dst.at[some], send_sem=e_send.at[i, step], recv_sem=e_recv.at[i, step],
+                device_id=(head, ctx - 1), device_id_type=MESH,
+            )
+            for i, (src, dst) in enumerate([(db, pdb), (g_ref, pg)])
+        ]
+
+    gives = jnp.logical_and(jnp.logical_not(even), ctx < nc - 1)
+    composes = jnp.logical_and(even, ctx < nc - 2)
 
     def local_step(step, carry):
         heads, lds, strengths = [], [], []
@@ -254,9 +280,16 @@
             columns = pl.ds(pl.multiple_of(h * DV, DV), DV)
             qe_ref[:, columns] = qe
             o_ref[:, columns] = o
-            d_ref[h] = d.astype(BF16)
+            d_ref[h] = d
             g_ref[h] = jnp.broadcast_to(gl, (8, DV))
             bb_ref[h] = bb
+            db[h] = jnp.concatenate([d, bb], axis=1).astype(BF16)
+
+        @pl.when(gives)
+        def _():
+            for copy in pair_copies(step):
+                copy.start()
+
         return carry
 
     lax.fori_loop(0, khl // group, local_step, 0)
@@ -270,25 +303,61 @@
             device_id=(head, ctx + 1), device_id_type=MESH,
         )
 
-    @pl.when(ctx < nc - 1)
-    def _():
-        def relay(h, carry):
-            @pl.when(ctx > 0)
+    def forward_copy(h):
+        return pltpu.make_async_remote_copy(
+            src_ref=f_out.at[h], dst_ref=s_in.at[h], send_sem=f_send.at[h], recv_sem=f_recv.at[h],
+            device_id=(head, ctx + 2), device_id_type=MESH,
+        )
+
+    def relay_step(step, carry):
+        @pl.when(composes)
+        def _():
+            for copy in pair_copies(step):
+                copy.wait_recv()
+
+        def relay(t, inner):
+            h = step * per_step + t
+            g0 = g_ref[h][0:1, :]
+
+            @pl.when(composes)
             def _():
-                state_copy(h).wait_recv()
+                g1 = pg[h][0:1, :]
+                later = pdb[h]
+                d1 = later[:, :DK]
+                both = mm1(d1, db[h])
+                pair_d = (g1 * d_ref[h] + g0 * d1.astype(F32) - both[:, :DK]).astype(BF16)
+                pair_b = later[:, DK:].astype(F32) + g1 * bb_ref[h] - both[:, DK:]
+
+                @pl.when(ctx > 0)
+                def _():
+                    forward_copy(h).wait_recv()
+
+                state = s_in[h]
+                moved = (g1 * g0 * state.astype(F32) + pair_b) - mm1(pair_d, state)
+                f_out[h] = moved.astype(BF16)
+                forward_copy(h).start()
+
+            @pl.when(ctx == nc - 2)
+            def _():
+                if nc > 2:
+                    forward_copy(h).wait_recv()
 
             state = s_in[h]
-            moved = (g_ref[h][0:1, :] * state.astype(F32) + bb_ref[h]) - mm1(d_ref[h], state)
+            moved = (g0 * state.astype(F32) + bb_ref[h]) - mm1(db[h][:, :DK], state)
             s_out[h] = moved.astype(BF16)
             state_copy(h).start()
-            return carry
-
-        lax.fori_loop(0, vhl, relay, 0)
+            return inner
+
+        return lax.fori_loop(0, per_step, relay, carry)
+
+    @pl.when(even)
+    def _():
+        lax.fori_loop(0, khl // group, relay_step, 0)
 
     loads[10].wait()
 
     def finish_pair(p):
-        @pl.when(ctx == nc - 1)
+        @pl.when(jnp.logical_not(even))
         def _():
             for r in range(RATIO):
                 state_copy(p * RATIO + r).wait_recv()
@@ -353,13 +422,30 @@
 
     @pl.when(ctx < nc - 1)
     def _():
+        for halo in halos:
+            halo.wait_send()
+
+    @pl.when(even)
+    def _():
         def drain(h, carry):
             state_copy(h).wait_send()
             return carry
 
         lax.fori_loop(0, vhl, drain, 0)
-        for halo in halos:
-            halo.wait_send()
+
+    @pl.when(composes)
+    def _():
+        def drain(h, carry):
+            forward_copy(h).wait_send()
+            return carry
+
+        lax.fori_loop(0, vhl, drain, 0)
+
+    @pl.when(gives)
+    def _():
+        for step in range(khl // group):
+            for copy in pair_copies(step):
+                copy.wait_send()
 
 
 def local(q_in, k_in, v_in, gate_in, conv_q, conv_k, value_conv_taps, a_in, b_in, a_log, dt_bias,
@@ -390,13 +476,17 @@
             vmem((n + 8, RATIO * DV), F32),
             vmem((n, vhl * DK), F32),
             vmem((n, vhl * DV), F32),
-            vmem((vhl, DK, DK), BF16),
+            vmem((vhl, DK, DK), F32),
             vmem((vhl, 8, DV), F32),
             vmem((vhl, DK, DV), F32),
             vmem((n, RATIO * DV), BF16),
             vmem((n, total_width), F32),
             vmem((vhl, DK, DV), BF16),
             vmem((vhl, DK, DV), BF16),
+            vmem((vhl, DK, DV), BF16),
+            vmem((vhl, DK, DK + DV), BF16),
+            vmem((vhl, DK, DK + DV), BF16),
+            vmem((vhl, 8, DV), F32),
             vmem((n, width), F32),
             vmem((nx, n, width), BF16),
             vmem((nx, n, width), BF16),
@@ -407,6 +497,10 @@
             dma((3,)),
             dma((vhl,)),
             dma((vhl,)),
+            dma((vhl,)),
+            dma((vhl,)),
+            dma((2, khl)),
+            dma((2, khl)),
             dma((nx,)),
             dma((nx,)),
             dma((nx - 1,)),

time: 48.6 us -> 47.2 us (0.971)
  Pallas kernels: 46.8 us -> 45.4 us
    pallas_call x1, Pallas kernels: 46.8 us -> 45.4 us  [local(): pl.pallas_call(functools.partial(body, nh, nc), in_specs=[smem, smem] + [...]
where the time goes in v4:
time: 47.2 us; the launch traced here: 47 us
  Pallas kernels  45.4 us (96%)
  local copies, waits for them, and re-layouts  1.67 us (4%)
    pallas_call x1, Pallas kernels, local(): pl.pallas_call(functools.partial(body, nh, nc), in_specs=[smem, smem] + [...  45.4 us
    unnamed x1, local copies, waits for them, and re-layouts  1.67 us

profile of v4, /device:TPU:29, one launch (start us, length us, event | category | flops | bytes accessed | tf_op | source)
XLA Modules:
  0.0 47.0 jit_solution(6802850266164345654)
XLA Ops:
  0.0 45.4 %shard_map.127 = bf16[256,512]{1,0:T(8,128)(2,1)} custom-call(f32[8]{0:T(128)} %alog_ref.1, f32[8]{0:T(128)} %dt_ref.1, bf16[256,512]{1,0:T(8,128)(2,1)} %q_hbm.1, bf16[256,512]{1,0:T(8,128)(2,1)} %k_hbm.1, bf16[256,1024]{1,0:T(8,128)(2,1)} %v_hbm.1, f32[4,512]{1,0:T(4,128)} %cq_hbm.1, f32[4,512]{1,0:T(4,128)} %ck_hbm.1, f32[4,1024]{1,0:T(4,128)} %cv_hbm.1, ...), custom_call_target="tpu_custom_call" | custom-call | tf_op jit(solution)/shard_map/pallas_call | solution.py:467
  45.4 1.7 %copy.15 = bf16[256,512]{1,0:T(8,128)(2,1)} copy(bf16[256,512]{1,0:T(8,128)(2,1)} %shard_map.127) | data formatting | bytes 524288

commit v5 on v4

--- a/solution.py
+++ b/solution.py
@@ -310,49 +310,54 @@
         )
 
     def relay_step(step, carry):
-        @pl.when(composes)
-        def _():
-            for copy in pair_copies(step):
-                copy.wait_recv()
+        for copy in pair_copies(step):
+            copy.wait_recv()
+
+        for t in range(per_step):
+            h = step * per_step + t
+            g1 = pg[h][0:1, :]
+            later = pdb[h]
+            d1 = later[:, :DK]
+            both = mm1(d1, db[h])
+            pair_d = (g1 * d_ref[h] + g_ref[h][0:1, :] * d1.astype(F32) - both[:, :DK]).astype(BF16)
+            pdb[h, :, :DK] = pair_d
+            d_ref[h] = later[:, DK:].astype(F32) + g1 * bb_ref[h] - both[:, DK:]
 
         def relay(t, inner):
             h = step * per_step + t
-            g0 = g_ref[h][0:1, :]
-
-            @pl.when(composes)
+
+            @pl.when(ctx > 0)
             def _():
-                g1 = pg[h][0:1, :]
-                later = pdb[h]
-                d1 = later[:, :DK]
-                both = mm1(d1, db[h])
-                pair_d = (g1 * d_ref[h] + g0 * d1.astype(F32) - both[:, :DK]).astype(BF16)
-                pair_b = later[:, DK:].astype(F32) + g1 * bb_ref[h] - both[:, DK:]
-
-                @pl.when(ctx > 0)
-                def _():
-                    forward_copy(h).wait_recv()
-
-                state = s_in[h]
-                moved = (g1 * g0 * state.astype(F32) + pair_b) - mm1(pair_d, state)
-                f_out[h] = moved.astype(BF16)
-                forward_copy(h).start()
-
+                forward_copy(h).wait_recv()
+
+            state = s_in[h]
+            decay = pg[h][0:1, :] * g_ref[h][0:1, :]
+            moved = (decay * state.astype(F32) + d_ref[h]) - mm1(pdb[h][:, :DK], state)
+            f_out[h] = moved.astype(BF16)
+            forward_copy(h).start()
+            return inner
+
+        return lax.fori_loop(0, per_step, relay, carry)
+
+    @pl.when(composes)
+    def _():
+        lax.fori_loop(0, khl // group, relay_step, 0)
+
+    def hand_over(h, carry):
+        if nc > 2:
             @pl.when(ctx == nc - 2)
             def _():
-                if nc > 2:
-                    forward_copy(h).wait_recv()
-
-            state = s_in[h]
-            moved = (g0 * state.astype(F32) + bb_ref[h]) - mm1(db[h][:, :DK], state)
-            s_out[h] = moved.astype(BF16)
-            state_copy(h).start()
-            return inner
-
-        return lax.fori_loop(0, per_step, relay, carry)
+                forward_copy(h).wait_recv()
+
+        state = s_in[h]
+        moved = (g_ref[h][0:1, :] * state.astype(F32) + bb_ref[h]) - mm1(db[h][:, :DK], state)
+        s_out[h] = moved.astype(BF16)
+        state_copy(h).start()
+        return carry
 
     @pl.when(even)
     def _():
-        lax.fori_loop(0, khl // group, relay_step, 0)
+        lax.fori_loop(0, vhl, hand_over, 0)
 
     loads[10].wait()
 

time: 47.2 us -> 47.1 us (level)
  no operation moved by 1% of the time
where the time goes in v5:
time: 47.1 us; the launch traced here: 46.8 us
  Pallas kernels  45.1 us (96%)
  local copies, waits for them, and re-layouts  1.67 us (4%)
    pallas_call x1, Pallas kernels, local(): pl.pallas_call(functools.partial(body, nh, nc), in_specs=[smem, smem] + [...  45.1 us
    unnamed x1, local copies, waits for them, and re-layouts  1.67 us

profile of v5, /device:TPU:29, one launch (start us, length us, event | category | flops | bytes accessed | tf_op | source)
XLA Modules:
  0.0 46.8 jit_solution(5135558831584769989)
XLA Ops:
  0.0 45.1 %shard_map.127 = bf16[256,512]{1,0:T(8,128)(2,1)} custom-call(f32[8]{0:T(128)} %alog_ref.1, f32[8]{0:T(128)} %dt_ref.1, bf16[256,512]{1,0:T(8,128)(2,1)} %q_hbm.1, bf16[256,512]{1,0:T(8,128)(2,1)} %k_hbm.1, bf16[256,1024]{1,0:T(8,128)(2,1)} %v_hbm.1, f32[4,512]{1,0:T(4,128)} %cq_hbm.1, f32[4,512]{1,0:T(4,128)} %ck_hbm.1, f32[4,1024]{1,0:T(4,128)} %cv_hbm.1, ...), custom_call_target="tpu_custom_call" | custom-call | tf_op jit(solution)/shard_map/pallas_call | solution.py:472
  45.1 1.7 %copy.15 = bf16[256,512]{1,0:T(8,128)(2,1)} copy(bf16[256,512]{1,0:T(8,128)(2,1)} %shard_map.127) | data formatting | bytes 524288
